TPU v7x, 128 devices: a whole 4x4x4 slice. The times are simulated.
128 devices in a mesh: seq: 16 (over x_lo, y, core), tp: 8 (over x_hi, z).
Axes of the slice: x: 4 (x_hi: 2, x_lo: 2; x = x_hi * 2 + x_lo), y: 4, z: 4, core: 2. Of those that a mesh axis runs over, the one named last changes fastest.
Arguments:
- embeddings: bfloat16 [6144, 4096], P('seq', 'tp'), may hold values from -6 to 6
- span_mask: int32 [6144], P('seq'), may hold values from 0 to 1, as said below
- sentinel_id: int32 [6144], P('seq'), may hold values from 0 to 99, as said below
- sentinel_table: bfloat16 [100, 4096], P(None, 'tp'), may hold values from -6 to 6
- gen_weight: bfloat16 [4096, 240], P(None, 'tp'), may hold values from -0.1875 to 0.1875
- up_weight: bfloat16 [4096, 8192], P(None, 'tp'), may hold values from -0.09375 to 0.09375
- down_weight: bfloat16 [8192, 4096], P('tp'), may hold values from -0.0625 to 0.0625
- cotangent: bfloat16 [6144, 4096], P('seq', 'tp'), may hold values from -0.59765625 to 0.59765625
Outputs:
- layer_output: bfloat16 [6144, 4096], P('seq', 'tp')
- embed_grad: float32 [6144, 4096], P('seq', 'tp')
- table_grad: float32 [100, 4096], P(None, 'tp')
- gen_grad: float32 [4096, 240], P(None, 'tp')
- up_grad: float32 [4096, 8192], P('seq', 'tp')
- down_grad: float32 [8192, 4096], P('tp', 'seq')
Inputs may be any that keep to these rules, and one draw needn't show every extreme that they name: `span_mask`: the tokens fall into aligned blocks of 16; each block holds exactly one span of 1 to 3 consecutive tokens marked 1, the rest 0. `sentinel_id`: all 16 tokens of an aligned block carry the same sentinel id.
All inputs are finite; a program needn't handle non-finite values.
Results may differ from a plain program's by a relative error of at most 0.035.
Values may be sent and summed in bfloat16 or wider, within the bound.
No kernel may reach another device: no remote copies, remote signals or barrier semaphores. Data moves between devices by JAX's collectives and lax.ppermute only.
A program may use at most 192 MiB of HBM per device.

v0:
```python
import jax
import jax.numpy as jnp
from jax import lax
from jax.sharding import PartitionSpec as P

KW = 15
SENT = 100


def with_halo(block, sides, width):
    for axis, dim in sides:
        count = lax.axis_size(axis)
        forward = [(i, i + 1) for i in range(count - 1)]
        backward = [(target, source) for source, target in forward]
        low = lax.ppermute(
            lax.slice_in_dim(block, block.shape[dim] - width, None, axis=dim), axis, forward
        )
        high = lax.ppermute(lax.slice_in_dim(block, 0, width, axis=dim), axis, backward)
        block = jnp.concatenate([low, block, high], axis=dim)
    return block


def gelu_tanh(values):
    return jax.nn.gelu(values, approximate=True)


def body(
    embeddings,
    span_mask,
    sentinel_id,
    sentinel_table,
    gen_weight,
    up_weight,
    down_weight,
    cotangent,
):
    tok_rows, feat_width = embeddings.shape
    head_count = gen_weight.shape[1] // KW
    head_width = feat_width // head_count
    tap_reach = (KW - 1) // 2
    sentinel_codes = jnp.arange(SENT, dtype=jnp.int32)
    onehot = sentinel_id[:, None] == sentinel_codes[None, :]
    picked = jnp.dot(
        onehot.astype(jnp.bfloat16), sentinel_table, preferred_element_type=jnp.float32
    ).astype(jnp.bfloat16)
    masked = span_mask[:, None] == 1
    hidden = jnp.where(masked, picked, embeddings)
    full_hidden = lax.all_gather(hidden, "tp", axis=1, tiled=True)
    logits = jnp.dot(full_hidden, gen_weight, preferred_element_type=jnp.float32)
    exp_logits = jnp.exp(logits.reshape(tok_rows, head_count, KW))
    kernel = exp_logits / jnp.sum(exp_logits, axis=-1, keepdims=True)
    padded = with_halo(hidden, (("seq", 0),), tap_reach)
    padded = padded.reshape(tok_rows + 2 * tap_reach, head_count, head_width)
    conv_sum = jnp.zeros((tok_rows, head_count, head_width), jnp.float32)
    for tap_index in range(KW):
        conv_sum = (
            conv_sum + kernel[:, :, tap_index, None] * padded[tap_index : tap_index + tok_rows]
        )
    act = (hidden.astype(jnp.float32) + conv_sum.reshape(tok_rows, feat_width)).astype(jnp.bfloat16)
    shard_piece = lax.all_gather(act, "tp", axis=1, tiled=True)
    up_rows = up_weight
    pre_sum = jnp.dot(shard_piece, up_rows, preferred_element_type=jnp.float32)
    full_copy = shard_piece
    middle, gelu_back = jax.vjp(gelu_tanh, pre_sum)
    middle = middle.astype(jnp.bfloat16)
    down_cols = down_weight
    ffn_total = lax.psum_scatter(
        lax.dot_general(
            down_cols, middle, (((0,), (1,)), ((), ())), preferred_element_type=jnp.float32
        ).astype(jnp.bfloat16),
        "tp",
        scatter_dimension=0,
        tiled=True,
    ).astype(jnp.float32)
    layer_output = (act.astype(jnp.float32) + ffn_total.T).astype(jnp.bfloat16)
    shard_piece = lax.all_gather(cotangent, "tp", axis=1, tiled=True)
    down_cols = down_weight
    middle_sum = lax.dot_general(
        shard_piece, down_cols, (((1,), (1,)), ((), ())), preferred_element_type=jnp.float32
    )
    block_term = lax.dot_general(
        middle, shard_piece, (((0,), (0,)), ((), ())), preferred_element_type=jnp.float32
    )
    down_term = block_term
    middle_grad, down_term = (middle_sum, down_term)
    down_grad = lax.psum_scatter(
        down_term.astype(jnp.bfloat16), "seq", scatter_dimension=1, tiled=True
    ).astype(jnp.float32)
    pre_grad = gelu_back(middle_grad)[0].astype(jnp.bfloat16)
    up_grad = lax.psum_scatter(
        lax.dot_general(
            full_copy, pre_grad, (((0,), (0,)), ((), ())), preferred_element_type=jnp.float32
        ).astype(jnp.bfloat16),
        "seq",
        scatter_dimension=0,
        tiled=True,
    ).astype(jnp.float32)
    up_rows = up_weight
    act_back = lax.psum_scatter(
        lax.dot_general(
            up_rows, pre_grad, (((1,), (1,)), ((), ())), preferred_element_type=jnp.float32
        ).astype(jnp.bfloat16),
        "tp",
        scatter_dimension=0,
        tiled=True,
    ).astype(jnp.float32)
    act_grad = cotangent.astype(jnp.float32) + act_back.T
    act_three = act_grad.reshape(tok_rows, head_count, head_width)
    kernel_grad = jnp.stack(
        [
            jnp.sum(act_three * padded[tap_index : tap_index + tok_rows], axis=-1)
            for tap_index in range(KW)
        ],
        axis=-1,
    )
    weighted = jnp.sum(kernel * kernel_grad, axis=-1, keepdims=True)
    logit_grad = (
        (kernel * (kernel_grad - weighted)).reshape(tok_rows, head_count * KW).astype(jnp.bfloat16)
    )
    joined = jnp.concatenate([act_grad, kernel.reshape(tok_rows, head_count * KW)], axis=1)
    joined_pad = with_halo(joined.astype(jnp.bfloat16), (("seq", 0),), tap_reach).astype(
        joined.dtype
    )
    grad_pad = joined_pad[:, :feat_width].reshape(tok_rows + 2 * tap_reach, head_count, head_width)
    kernel_pad = joined_pad[:, feat_width:].reshape(tok_rows + 2 * tap_reach, head_count, KW)
    conv_back = jnp.zeros((tok_rows, head_count, head_width), jnp.float32)
    for tap_index in range(KW):
        lower = 2 * tap_reach - tap_index
        conv_back = (
            conv_back
            + kernel_pad[lower : lower + tok_rows, :, tap_index, None]
            * grad_pad[lower : lower + tok_rows]
        )
    gen_part = lax.dot_general(
        full_hidden, logit_grad, (((0,), (0,)), ((), ())), preferred_element_type=jnp.float32
    )
    gen_back = (
        lax.psum_scatter(
            lax.dot_general(
                gen_weight, logit_grad, (((1,), (1,)), ((), ())), preferred_element_type=jnp.float32
            ).astype(jnp.bfloat16),
            "tp",
            scatter_dimension=0,
            tiled=True,
        )
        .astype(jnp.float32)
        .T
    )
    hidden_grad = act_grad + conv_back.reshape(tok_rows, feat_width) + gen_back
    embed_grad = jnp.where(masked, jnp.float32(0.0), hidden_grad)
    table_part = jnp.dot(
        onehot.astype(jnp.float32).T,
        jnp.where(masked, hidden_grad, jnp.float32(0.0)),
        precision=lax.Precision.HIGHEST,
    )
    gen_sum, table_grad = (
        lax.psum(gen_part.astype(jnp.bfloat16), "seq").astype(jnp.float32),
        lax.psum(table_part.astype(jnp.bfloat16), "seq").astype(jnp.float32),
    )
    return (layer_output, embed_grad, table_grad, gen_sum, up_grad, down_grad)


def solution(mesh):
    placed = (
        P("seq", "tp"),
        P("seq"),
        P("seq"),
        P(None, "tp"),
        P(None, "tp"),
        P(None, "tp"),
        P("tp", None),
        P("seq", "tp"),
    )
    return jax.shard_map(
        body,
        mesh=mesh,
        in_specs=placed,
        out_specs=(
            P("seq", "tp"),
            P("seq", "tp"),
            P(None, "tp"),
            P(None, "tp"),
            P("seq", "tp"),
            P("tp", "seq"),
        ),
        check_vma=False,
    )
```

profile of v0, /device:TPU:0, one launch (start us, length us, event | category | flops | bytes accessed | tf_op | source)
XLA Modules:
  0.0 786.1 jit_solution(15642379624280598113)
XLA Ops:
  7.9 2.1 fusion.11
  11.6 1.3 collective-permute-start
  12.9 1.3 collective-permute-start.1
  14.2 63.1 %all-gather.4.cloned.1.call-done = bf16[384,4096]{1,0:T(8,128)(2,1)} async-done(((bf16[384,512]{1,0:T(8,128)(2,1)}), bf16[384,4096]{1,0:T(8,128)(2,1)}) %all-gather.4.cloned.1.call-update) | async-done | bytes 3145744 | tf_op jit(solution)/shard_map/all_gather | solution.py:48
  77.3 2.9 convolution_exponential_fusion
  91.1 2.5 fusion.45
  93.8 47.6 %all-gather.8.cloned.1.call-done = bf16[384,4096]{1,0:T(8,128)(2,1)} async-done(((bf16[384,512]{1,0:T(8,128)(2,1)}), bf16[384,4096]{1,0:T(8,128)(2,1)}) %all-gather.8.cloned.1.call-update) | async-done | bytes 3145744 | tf_op jit(solution)/shard_map/all_gather | solution.py:76
  141.4 6.8 fusion.69
  148.3 57.8 %all-gather.6.cloned.1.call-done = bf16[384,4096]{1,0:T(8,128)(2,1)} async-done(((bf16[384,512]{1,0:T(8,128)(2,1)}), bf16[384,4096]{1,0:T(8,128)(2,1)}) %all-gather.6.cloned.1.call-update) | async-done | bytes 3145744 | tf_op jit(solution)/shard_map/all_gather | solution.py:60
  206.1 9.7 %fusion.10 = (bf16[384,1024]{1,0:T(8,128)(2,1)S(1)}, f32[384,1024]{1,0:T(8,128)}) fusion(f32[384,1024]{1,0:T(8,128)S(1)} %fusion.69, bf16[384,4096]{1,0:T(8,128)(2,1)} %all-gather.6.cloned.1.call-done, bf16[4096,1024]{1,0:T(8,128)(2,1)} %param.13), kind=kOutput, calls=%fused_computation.18 | convolution fusion | flops 3229089792 | bytes 15466496 | tf_op jit(solution)/shard_map/dot_general | solution.py:62
  215.7 10.6 %fusion.2 = bf16[4096,384]{0,1:T(8,128)(2,1)} fusion(bf16[384,1024]{1,0:T(8,128)(2,1)S(1)} %get-tuple-element.62, bf16[4096,1024]{1,0:T(8,128)(2,1)} %param.13), kind=kOutput, calls=%fused_computation.7 | convolution fusion | flops 3222798336 | bytes 12320768 | tf_op jit(solution)/shard_map/dot_general | solution.py:100
  226.9 76.9 %reduce-scatter.8.cloned.1.call-done = bf16[512,384]{0,1:T(8,128)(2,1)} async-done(((bf16[4096,384]{0,1:T(8,128)(2,1)}), bf16[512,384]{0,1:T(8,128)(2,1)}) %reduce-scatter.8.cloned.1.call-update) | async-done | bytes 393232 | tf_op jit(solution)/shard_map/reduce_scatter | solution.py:99
  303.8 3.5 convert_multiply_fusion.16
  307.3 1.6 mul.679
  309.5 1.7 mul.667
  311.8 1.7 mul.669
  314.0 1.7 mul.671
  316.2 1.7 mul.673
  318.4 1.7 mul.675
  321.8 2.7 convert_multiply_fusion.2
  324.5 1.6 mul.695
  326.7 1.7 mul.683
  328.9 1.7 mul.685
  331.3 1.7 mul.687
  333.5 1.7 mul.689
  335.8 1.7 mul.691
  340.6 2.7 fusion.3
  343.3 1.3 copy-done.18
  344.7 8.3 %fusion.1 = bf16[4096,384]{0,1:T(8,128)(2,1)} fusion(bf16[1024,4096]{1,0:T(8,128)(2,1)} %param.14, f32[384,1024]{1,0:T(8,128)S(1)} %copy-done.18), kind=kOutput, calls=%fused_computation.6 | convolution fusion | flops 3226337280 | bytes 13107200 | tf_op jit(solution)/shard_map/dot_general | solution.py:68
  354.1 1.3 collective-permute-start.2
  355.4 1.6 collective-permute-start.3
  357.0 1.3 convolution_convert_fusion.5
  358.4 1.9 collective-permute-done.3
  387.8 33.8 %reduce-scatter.10.cloned.1.call-done = bf16[512,384]{0,1:T(8,128)(2,1)} async-done(((bf16[4096,384]{0,1:T(8,128)(2,1)}), bf16[512,384]{0,1:T(8,128)(2,1)}) %reduce-scatter.10.cloned.1.call-update) | async-done | bytes 393232 | tf_op jit(solution)/shard_map/reduce_scatter | solution.py:138
  421.6 5.9 broadcast_select_fusion
  427.6 1.3 convolution_convert_fusion.7
  429.1 10.3 %convolution_convert_fusion = bf16[1024,4096]{1,0:T(8,128)(2,1)} fusion(bf16[384,4096]{1,0:T(8,128)(2,1)} %all-gather.8.cloned.1.call-done, f32[384,1024]{1,0:T(8,128)} %get-tuple-element.63), kind=kOutput, calls=%fused_computation.1 | convolution fusion | flops 3228958720 | bytes 13107200 | tf_op jit(solution)/shard_map/dot_general | solution.py:81
  439.5 1.8 copy-done.17
  441.4 7.9 %convolution_convert_fusion.1 = bf16[4096,1024]{1,0:T(8,128)(2,1)} fusion(bf16[384,4096]{1,0:T(8,128)(2,1)S(1)} %copy-done.17, bf16[384,1024]{1,0:T(8,128)(2,1)} %copy-done.19), kind=kOutput, calls=%fused_computation.2 | convolution fusion | flops 3225419776 | bytes 12320768 | tf_op jit(solution)/shard_map/dot_general | solution.py:91
  449.2 54.4 %reduce-scatter.6.cloned.1.call-done = bf16[512,384]{0,1:T(8,128)(2,1)} async-done(((bf16[4096,384]{0,1:T(8,128)(2,1)}), bf16[512,384]{0,1:T(8,128)(2,1)}) %reduce-scatter.6.cloned.1.call-update) | async-done | bytes 393232 | tf_op jit(solution)/shard_map/reduce_scatter | solution.py:67
  503.6 1.8 fusion.43
  505.5 117.2 %all-reduce.3.cloned.1.call-done = (bf16[100,512]{1,0:T(8,128)(2,1)}, bf16[4096,30]{0,1:T(8,128)(2,1)}) async-done(((bf16[100,512]{1,0:T(8,128)(2,1)}, bf16[4096,30]{0,1:T(8,128)(2,1)}), (bf16[100,512]{1,0:T(8,128)(2,1)}, bf16[4096,30]{0,1:T(8,128)(2,1)})) %all-reduce.3.cloned.1.call-update) | async-done | bytes 348176 | tf_op jit(solution)/shard_map/psum | solution.py:158
  622.6 1.6 convert_element_type.197
  624.2 1.8 convert_element_type.199
  626.1 75.2 %reduce-scatter.14.cloned.1.call-done = bf16[1024,256]{1,0:T(8,128)(2,1)} async-done(((bf16[1024,4096]{1,0:T(8,128)(2,1)}), bf16[1024,256]{1,0:T(8,128)(2,1)}) %reduce-scatter.14.cloned.1.call-update) | async-done | bytes 524304 | tf_op jit(solution)/shard_map/reduce_scatter | solution.py:86
  701.3 2.1 convert_element_type.203
  703.4 73.6 %reduce-scatter.12.cloned.1.call-done = bf16[256,1024]{1,0:T(8,128)(2,1)} async-done(((bf16[4096,1024]{1,0:T(8,128)(2,1)}), bf16[256,1024]{1,0:T(8,128)(2,1)}) %reduce-scatter.12.cloned.1.call-update) | async-done | bytes 524304 | tf_op jit(solution)/shard_map/reduce_scatter | solution.py:90
  777.0 2.1 convert_element_type.201
  (201 shorter events, 52.9 us)
Async XLA Ops:
  7.2 70.2 %copy-start = (bf16[4096,30]{0,1:T(8,128)(2,1)S(1)}, bf16[4096,30]{0,1:T(8,128)(2,1)}, u32[]{:S(2)}) copy-start(bf16[4096,30]{0,1:T(8,128)(2,1)} %param.12) | copy-start | bytes 737284
  7.2 70.2 %all-gather.4.cloned.1.call-start = ((), (), s32[]{:S(2)}) async-start(), calls=%async_computation.5 | async-start | bytes 3538944 | tf_op jit(solution)/shard_map/all_gather | solution.py:48
  10.1 131.3 %all-gather.8.cloned.1.call-start = ((), (), s32[]{:S(2)}) async-start(), calls=%async_computation.8 | async-start | bytes 3538944 | tf_op jit(solution)/shard_map/all_gather | solution.py:76
  10.9 195.2 %all-gather.6.cloned.1.call-start = ((), (), s32[]{:S(2)}) async-start(), calls=%async_computation.6 | async-start | bytes 3538944 | tf_op jit(solution)/shard_map/all_gather | solution.py:60
  11.6 79.0 %collective-permute-start = (bf16[7,512]{1,0:T(8,128)(2,1)S(1)}, bf16[7,512]{1,0:T(8,128)(2,1)S(1)}, u32[]{:S(2)}, u32[]{:S(2)}) collective-permute-start(bf16[7,512]{1,0:T(8,128)(2,1)S(1)} %get-tuple-element.28), channel_id=1, source_target_pairs={{0,8},{8,16},{16,24},{24,32},{32,40},{40,48},{48,56},{56,64},{64,7... | collective-permute-start | bytes 21512 | tf_op jit(solution)/shard_map/ppermute | solution.py:15
  12.9 77.7 %collective-permute-start.1 = (bf16[7,512]{1,0:T(8,128)(2,1)S(1)}, bf16[7,512]{1,0:T(8,128)(2,1)S(1)}, u32[]{:S(2)}, u32[]{:S(2)}) collective-permute-start(bf16[7,512]{1,0:T(8,128)(2,1)S(1)} %get-tuple-element.29), channel_id=1, source_target_pairs={{8,0},{16,8},{24,16},{32,24},{40,32},{48,40},{56,48},{64,56},{72,6... | collective-permute-start | bytes 21512 | tf_op jit(solution)/shard_map/ppermute | solution.py:18
  90.1 1.0 copy-start.3
  93.6 210.2 %reduce-scatter.8.cloned.1.call-start = ((), (), s32[]{:S(2)}) async-start(), calls=%async_computation.9 | async-start | bytes 3538944 | tf_op jit(solution)/shard_map/reduce_scatter | solution.py:99
  215.7 10.6 %copy-start.19 = (bf16[384,1024]{1,0:T(8,128)(2,1)}, bf16[384,1024]{1,0:T(8,128)(2,1)S(1)}, u32[]{:S(2)}) copy-start(bf16[384,1024]{1,0:T(8,128)(2,1)S(1)} %get-tuple-element.62) | copy-start | bytes 2359300
  226.4 77.4 %copy-start.4 = (bf16[384,512]{1,0:T(8,128)(2,1)S(1)}, bf16[384,512]{1,0:T(8,128)(2,1)}, u32[]{:S(2)}) copy-start(bf16[384,512]{1,0:T(8,128)(2,1)} %param.15) | copy-start | bytes 1179652
  226.4 195.2 %reduce-scatter.10.cloned.1.call-start = ((), (), s32[]{:S(2)}) async-start(), calls=%async_computation.10 | async-start | bytes 3538944 | tf_op jit(solution)/shard_map/reduce_scatter | solution.py:138
  320.6 1.2 copy-start.7
  343.3 1.4 copy-start.18
  343.3 160.3 %reduce-scatter.6.cloned.1.call-start = ((), (), s32[]{:S(2)}) async-start(), calls=%async_computation.7 | async-start | bytes 3538944 | tf_op jit(solution)/shard_map/reduce_scatter | solution.py:67
  353.0 4.0 copy-start.2
  353.0 269.6 %all-reduce.3.cloned.1.call-start = ((), (), s32[]{:S(2)}) async-start(), calls=%async_computation.13 | async-start | bytes 737280 | tf_op jit(solution)/shard_map/psum | solution.py:158
  354.1 4.3 collective-permute-start.2
  355.4 5.0 copy-start.9
  355.4 4.9 collective-permute-start.3
  367.1 0.9 copy-start.15
  367.6 1.8 copy-start.14
  369.4 1.5 copy-start.13
  370.9 1.4 copy-start.12
  372.3 1.4 copy-start.11
  373.7 1.4 copy-start.10
  386.4 35.2 %copy-start.5 = (bf16[384,512]{1,0:T(8,128)(2,1)S(1)}, bf16[384,512]{1,0:T(8,128)(2,1)}, u32[]{:S(2)}) copy-start(bf16[384,512]{1,0:T(8,128)(2,1)} %param.15) | copy-start | bytes 1179652
  386.4 35.2 %copy-start.8 = (bf16[512,384]{0,1:T(8,128)(2,1)S(1)}, bf16[512,384]{0,1:T(8,128)(2,1)}, u32[]{:S(2)}) copy-start(bf16[512,384]{0,1:T(8,128)(2,1)} %reduce-scatter.8.cloned.1.call-done) | copy-start | bytes 1179652
  421.6 5.9 copy-start.16
  428.8 272.5 %reduce-scatter.14.cloned.1.call-start = ((), (), s32[]{:S(2)}) async-start(), calls=%async_computation.12 | async-start | bytes 8912896 | tf_op jit(solution)/shard_map/reduce_scatter | solution.py:86
  439.4 1.9 copy-start.17
  439.5 337.6 %reduce-scatter.12.cloned.1.call-start = ((), (), s32[]{:S(2)}) async-start(), calls=%async_computation.11 | async-start | bytes 8912896 | tf_op jit(solution)/shard_map/reduce_scatter | solution.py:90
  449.2 54.4 %copy-start.6 = (bf16[384,512]{1,0:T(8,128)(2,1)S(1)}, bf16[384,512]{1,0:T(8,128)(2,1)}, u32[]{:S(2)}) copy-start(bf16[384,512]{1,0:T(8,128)(2,1)} %fusion.45) | copy-start | bytes 1179652
  624.2 154.9 %copy-start.1 = (bf16[4096,30]{0,1:T(8,128)(2,1)S(1)}, bf16[4096,30]{0,1:T(8,128)(2,1)}, u32[]{:S(2)}) copy-start(bf16[4096,30]{0,1:T(8,128)(2,1)} %param.12) | copy-start | bytes 737284
Sparse Core Ops, SparseCore 0:
  10.8 66.5 all-gather.3
  79.5 61.8 all-gather.7
  144.2 61.8 all-gather.5
  226.5 77.2 reduce-scatter.7
  343.4 78.1 reduce-scatter.9
  425.3 78.2 reduce-scatter.5
  506.7 115.8 all-reduce.2
  625.2 76.0 reduce-scatter.13
  703.9 73.1 reduce-scatter.11
where the time goes:
time: 795 us; the launch traced here: 786 us
  waiting for transfers between devices  602 us (76%)
  local copies, waits for them, and re-layouts  64.7 us (8%)
  matrix products  64 us (8%)
  other arithmetic  33.2 us (4%)
  between operations  15.1 us (2%)
    psum x1, waiting for transfers between devices, body(): lax.psum(table_part.astype(jnp.bfloat16), 'seq').astype(jnp.float32)  117 us
    reduce_scatter x1, waiting for transfers between devices, body(): lax.psum_scatter(lax.dot_general(up_rows, pre_grad, (((1,), (1,)), ((), (...  76.9 us
    reduce_scatter x1, waiting for transfers between devices, body(): lax.psum_scatter(down_term.astype(jnp.bfloat16), 'seq', scatter_dimension...  75.2 us
    reduce_scatter x1, waiting for transfers between devices, body(): lax.psum_scatter(lax.dot_general(full_copy, pre_grad, (((0,), (0,)), ((),...  73.6 us
    all_gather x1, waiting for transfers between devices, body(): full_hidden = lax.all_gather(hidden, 'tp', axis=1, tiled=True)  63.1 us
    all_gather x1, waiting for transfers between devices, body(): shard_piece = lax.all_gather(act, 'tp', axis=1, tiled=True)  57.8 us
    reduce_scatter x1, waiting for transfers between devices, body(): lax.psum_scatter(lax.dot_general(down_cols, middle, (((0,), (1,)), ((), (...  54.4 us
    all_gather x1, waiting for transfers between devices, body(): shard_piece = lax.all_gather(cotangent, 'tp', axis=1, tiled=True)  47.6 us
  transfers between devices with their start and end apart: 13, of which 10 were waited for; matrix products, arithmetic and copies ran while one was open for 12% of the time, Pallas kernels for 0%

commit v1 on v0

--- a/solution.py
+++ b/solution.py
@@ -5,6 +5,12 @@
 
 KW = 15
 SENT = 100
+
+
+def gather_and_add(x, mesh_axis):
+    parts = lax.all_gather(x, mesh_axis, axis=0, tiled=False)
+    total = parts.sum(axis=0)
+    return total
 
 
 def with_halo(block, sides, width):
@@ -155,7 +161,7 @@
     )
     gen_sum, table_grad = (
         lax.psum(gen_part.astype(jnp.bfloat16), "seq").astype(jnp.float32),
-        lax.psum(table_part.astype(jnp.bfloat16), "seq").astype(jnp.float32),
+        gather_and_add(table_part.astype(jnp.bfloat16), "seq").astype(jnp.float32),
     )
     return (layer_output, embed_grad, table_grad, gen_sum, up_grad, down_grad)
 

time: 795 us -> 829 us (1.043)
  waiting for transfers between devices: 602 us -> 635 us
    all_gather x0 -> x1, waiting for transfers between devices: none -> 35.2 us  [gather_and_add(): parts = lax.all_gather(x, mesh_axis, axis=0, tiled=False)]
    unnamed x70 -> x68, local copies, waits for them, and re-layouts: 18.1 us -> 18 us
  transfers between devices with their start and end apart: 13 -> 14, of which waited for: 10 -> 11; matrix products, arithmetic and copies ran while one was open for 12% -> 12% of each run, Pallas kernels for 0% -> 0%
where the time goes in v1:
time: 829 us; the launch traced here: 821 us
  waiting for transfers between devices  635 us (77%)
  local copies, waits for them, and re-layouts  64.6 us (8%)
  matrix products  63.9 us (8%)
  other arithmetic  34.9 us (4%)
  between operations  15.4 us (2%)
    psum x1, waiting for transfers between devices, body(): lax.psum(gen_part.astype(jnp.bfloat16), 'seq').astype(jnp.float32)  116 us
    reduce_scatter x1, waiting for transfers between devices, body(): lax.psum_scatter(lax.dot_general(up_rows, pre_grad, (((1,), (1,)), ((), (...  76.9 us
    reduce_scatter x1, waiting for transfers between devices, body(): lax.psum_scatter(down_term.astype(jnp.bfloat16), 'seq', scatter_dimension...  74.8 us
    reduce_scatter x1, waiting for transfers between devices, body(): lax.psum_scatter(lax.dot_general(full_copy, pre_grad, (((0,), (0,)), ((),...  73.6 us
    all_gather x1, waiting for transfers between devices, body(): full_hidden = lax.all_gather(hidden, 'tp', axis=1, tiled=True)  63.1 us
    all_gather x1, waiting for transfers between devices, body(): shard_piece = lax.all_gather(act, 'tp', axis=1, tiled=True)  57.8 us
    reduce_scatter x1, waiting for transfers between devices, body(): lax.psum_scatter(lax.dot_general(down_cols, middle, (((0,), (1,)), ((), (...  54.3 us
    all_gather x1, waiting for transfers between devices, body(): shard_piece = lax.all_gather(cotangent, 'tp', axis=1, tiled=True)  47.6 us
  transfers between devices with their start and end apart: 14, of which 11 were waited for; matrix products, arithmetic and copies ran while one was open for 12% of the time, Pallas kernels for 0%

profile of v1, /device:TPU:0, one launch (start us, length us, event | category | flops | bytes accessed | tf_op | source)
XLA Modules:
  0.0 820.5 jit_solution(16154581846238026128)
XLA Ops:
  7.9 2.1 fusion.11
  11.6 1.3 collective-permute-start
  12.9 1.3 collective-permute-start.1
  14.2 63.1 %all-gather.7.cloned.1.call-done = bf16[384,4096]{1,0:T(8,128)(2,1)} async-done(((bf16[384,512]{1,0:T(8,128)(2,1)}), bf16[384,4096]{1,0:T(8,128)(2,1)}) %all-gather.7.cloned.1.call-update) | async-done | bytes 3145744 | tf_op jit(solution)/shard_map/all_gather | solution.py:54
  77.3 2.9 convolution_exponential_fusion
  91.1 2.5 fusion.46
  93.8 47.6 %all-gather.11.cloned.1.call-done = bf16[384,4096]{1,0:T(8,128)(2,1)} async-done(((bf16[384,512]{1,0:T(8,128)(2,1)}), bf16[384,4096]{1,0:T(8,128)(2,1)}) %all-gather.11.cloned.1.call-update) | async-done | bytes 3145744 | tf_op jit(solution)/shard_map/all_gather | solution.py:82
  141.4 6.8 fusion.70
  148.3 57.8 %all-gather.9.cloned.1.call-done = bf16[384,4096]{1,0:T(8,128)(2,1)} async-done(((bf16[384,512]{1,0:T(8,128)(2,1)}), bf16[384,4096]{1,0:T(8,128)(2,1)}) %all-gather.9.cloned.1.call-update) | async-done | bytes 3145744 | tf_op jit(solution)/shard_map/all_gather | solution.py:66
  206.1 9.7 %fusion.10 = (bf16[384,1024]{1,0:T(8,128)(2,1)S(1)}, f32[384,1024]{1,0:T(8,128)}) fusion(f32[384,1024]{1,0:T(8,128)S(1)} %fusion.70, bf16[384,4096]{1,0:T(8,128)(2,1)} %all-gather.9.cloned.1.call-done, bf16[4096,1024]{1,0:T(8,128)(2,1)} %param.13), kind=kOutput, calls=%fused_computation.18 | convolution fusion | flops 3229089792 | bytes 15466496 | tf_op jit(solution)/shard_map/dot_general | solution.py:68
  215.7 10.6 %fusion.2 = bf16[4096,384]{0,1:T(8,128)(2,1)} fusion(bf16[384,1024]{1,0:T(8,128)(2,1)S(1)} %get-tuple-element.60, bf16[4096,1024]{1,0:T(8,128)(2,1)} %param.13), kind=kOutput, calls=%fused_computation.7 | convolution fusion | flops 3222798336 | bytes 12320768 | tf_op jit(solution)/shard_map/dot_general | solution.py:106
  226.9 76.9 %reduce-scatter.8.cloned.1.call-done = bf16[512,384]{0,1:T(8,128)(2,1)} async-done(((bf16[4096,384]{0,1:T(8,128)(2,1)}), bf16[512,384]{0,1:T(8,128)(2,1)}) %reduce-scatter.8.cloned.1.call-update) | async-done | bytes 393232 | tf_op jit(solution)/shard_map/reduce_scatter | solution.py:105
  303.8 3.5 convert_multiply_fusion.16
  307.3 1.6 mul.679
  309.5 1.7 mul.667
  311.7 1.7 mul.669
  314.0 1.7 mul.671
  316.2 1.7 mul.673
  318.4 1.7 mul.675
  321.8 2.7 convert_multiply_fusion.2
  324.5 1.6 mul.695
  326.6 1.7 mul.683
  328.9 1.7 mul.685
  331.3 1.7 mul.687
  333.5 1.7 mul.689
  335.7 1.7 mul.691
  340.5 2.7 fusion.3
  343.3 1.3 copy-done.17
  344.6 8.3 %fusion.1 = bf16[4096,384]{0,1:T(8,128)(2,1)} fusion(bf16[1024,4096]{1,0:T(8,128)(2,1)} %param.14, f32[384,1024]{1,0:T(8,128)S(1)} %copy-done.17), kind=kOutput, calls=%fused_computation.6 | convolution fusion | flops 3226337280 | bytes 13107200 | tf_op jit(solution)/shard_map/dot_general | solution.py:74
  354.0 1.3 collective-permute-start.2
  355.3 1.3 collective-permute-start.3
  356.6 1.3 convolution_convert_fusion.5
  358.2 1.9 collective-permute-done.3
  388.6 33.1 %reduce-scatter.10.cloned.1.call-done = bf16[512,384]{0,1:T(8,128)(2,1)} async-done(((bf16[4096,384]{0,1:T(8,128)(2,1)}), bf16[512,384]{0,1:T(8,128)(2,1)}) %reduce-scatter.10.cloned.1.call-update) | async-done | bytes 393232 | tf_op jit(solution)/shard_map/reduce_scatter | solution.py:144
  421.6 5.9 broadcast_select_fusion
  429.1 10.3 %convolution_convert_fusion = bf16[1024,4096]{1,0:T(8,128)(2,1)} fusion(bf16[384,4096]{1,0:T(8,128)(2,1)} %all-gather.11.cloned.1.call-done, f32[384,1024]{1,0:T(8,128)} %get-tuple-element.61), kind=kOutput, calls=%fused_computation.1 | convolution fusion | flops 3228958720 | bytes 13107200 | tf_op jit(solution)/shard_map/dot_general | solution.py:87
  439.5 1.8 copy-done.16
  441.4 7.9 convolution_convert_fusion.1
  449.2 54.3 %reduce-scatter.6.cloned.1.call-done = bf16[512,384]{0,1:T(8,128)(2,1)} async-done(((bf16[4096,384]{0,1:T(8,128)(2,1)}), bf16[512,384]{0,1:T(8,128)(2,1)}) %reduce-scatter.6.cloned.1.call-update) | async-done | bytes 393232 | tf_op jit(solution)/shard_map/reduce_scatter | solution.py:73
  503.6 1.8 fusion.44
  505.4 115.8 %all-reduce.2.cloned.1.call-done = bf16[4096,30]{0,1:T(8,128)(2,1)} async-done(((bf16[4096,30]{0,1:T(8,128)(2,1)}), bf16[4096,30]{0,1:T(8,128)(2,1)}) %all-reduce.2.cloned.1.call-update) | async-done | bytes 245776 | tf_op jit(solution)/shard_map/psum | solution.py:163
  621.2 1.8 convert_element_type.201
  623.0 35.2 %all-gather.13.cloned.1.call-done = bf16[16,100,512]{2,1,0:T(8,128)(2,1)} async-done(((bf16[1,100,512]{2,1,0:T(8,128)(2,1)}), bf16[16,100,512]{2,1,0:T(8,128)(2,1)}) %all-gather.13.cloned.1.call-update) | async-done | bytes 1638416 | tf_op jit(solution)/shard_map/all_gather | solution.py:11
  658.2 1.7 reduce_sum.182
  660.6 74.8 %reduce-scatter.14.cloned.1.call-done = bf16[1024,256]{1,0:T(8,128)(2,1)} async-done(((bf16[1024,4096]{1,0:T(8,128)(2,1)}), bf16[1024,256]{1,0:T(8,128)(2,1)}) %reduce-scatter.14.cloned.1.call-update) | async-done | bytes 524304 | tf_op jit(solution)/shard_map/reduce_scatter | solution.py:92
  735.4 2.1 convert_element_type.205
  737.5 73.6 %reduce-scatter.12.cloned.1.call-done = bf16[256,1024]{1,0:T(8,128)(2,1)} async-done(((bf16[4096,1024]{1,0:T(8,128)(2,1)}), bf16[256,1024]{1,0:T(8,128)(2,1)}) %reduce-scatter.12.cloned.1.call-update) | async-done | bytes 524304 | tf_op jit(solution)/shard_map/reduce_scatter | solution.py:96
  811.1 2.1 convert_element_type.203
  (203 shorter events, 56.1 us)
Async XLA Ops:
  7.2 70.2 %copy-start = (bf16[4096,30]{0,1:T(8,128)(2,1)S(1)}, bf16[4096,30]{0,1:T(8,128)(2,1)}, u32[]{:S(2)}) copy-start(bf16[4096,30]{0,1:T(8,128)(2,1)} %param.12) | copy-start | bytes 737284
  7.2 70.2 %all-gather.7.cloned.1.call-start = ((), (), s32[]{:S(2)}) async-start(), calls=%async_computation.5 | async-start | bytes 3538944 | tf_op jit(solution)/shard_map/all_gather | solution.py:54
  10.1 131.3 %all-gather.11.cloned.1.call-start = ((), (), s32[]{:S(2)}) async-start(), calls=%async_computation.8 | async-start | bytes 3538944 | tf_op jit(solution)/shard_map/all_gather | solution.py:82
  10.9 195.2 %all-gather.9.cloned.1.call-start = ((), (), s32[]{:S(2)}) async-start(), calls=%async_computation.6 | async-start | bytes 3538944 | tf_op jit(solution)/shard_map/all_gather | solution.py:66
  11.6 79.0 %collective-permute-start = (bf16[7,512]{1,0:T(8,128)(2,1)S(1)}, bf16[7,512]{1,0:T(8,128)(2,1)S(1)}, u32[]{:S(2)}, u32[]{:S(2)}) collective-permute-start(bf16[7,512]{1,0:T(8,128)(2,1)S(1)} %get-tuple-element.26), channel_id=1, source_target_pairs={{0,8},{8,16},{16,24},{24,32},{32,40},{40,48},{48,56},{56,64},{64,7... | collective-permute-start | bytes 21512 | tf_op jit(solution)/shard_map/ppermute | solution.py:21
  12.9 77.7 %collective-permute-start.1 = (bf16[7,512]{1,0:T(8,128)(2,1)S(1)}, bf16[7,512]{1,0:T(8,128)(2,1)S(1)}, u32[]{:S(2)}, u32[]{:S(2)}) collective-permute-start(bf16[7,512]{1,0:T(8,128)(2,1)S(1)} %get-tuple-element.27), channel_id=1, source_target_pairs={{8,0},{16,8},{24,16},{32,24},{40,32},{48,40},{56,48},{64,56},{72,6... | collective-permute-start | bytes 21512 | tf_op jit(solution)/shard_map/ppermute | solution.py:24
  90.1 1.0 copy-start.3
  93.6 210.2 %reduce-scatter.8.cloned.1.call-start = ((), (), s32[]{:S(2)}) async-start(), calls=%async_computation.9 | async-start | bytes 3538944 | tf_op jit(solution)/shard_map/reduce_scatter | solution.py:105
  215.7 10.6 %copy-start.18 = (bf16[384,1024]{1,0:T(8,128)(2,1)}, bf16[384,1024]{1,0:T(8,128)(2,1)S(1)}, u32[]{:S(2)}) copy-start(bf16[384,1024]{1,0:T(8,128)(2,1)S(1)} %get-tuple-element.60) | copy-start | bytes 2359300
  226.4 77.4 %copy-start.4 = (bf16[384,512]{1,0:T(8,128)(2,1)S(1)}, bf16[384,512]{1,0:T(8,128)(2,1)}, u32[]{:S(2)}) copy-start(bf16[384,512]{1,0:T(8,128)(2,1)} %param.15) | copy-start | bytes 1179652
  226.4 195.2 %reduce-scatter.10.cloned.1.call-start = ((), (), s32[]{:S(2)}) async-start(), calls=%async_computation.10 | async-start | bytes 3538944 | tf_op jit(solution)/shard_map/reduce_scatter | solution.py:144
  320.5 1.2 copy-start.7
  343.2 1.4 copy-start.17
  343.2 160.3 %reduce-scatter.6.cloned.1.call-start = ((), (), s32[]{:S(2)}) async-start(), calls=%async_computation.7 | async-start | bytes 3538944 | tf_op jit(solution)/shard_map/reduce_scatter | solution.py:73
  352.9 3.7 copy-start.2
  352.9 268.3 %all-reduce.2.cloned.1.call-start = ((), (), s32[]{:S(2)}) async-start(), calls=%async_computation.11 | async-start | bytes 524288 | tf_op jit(solution)/shard_map/psum | solution.py:163
  354.0 4.2 collective-permute-start.2
  355.3 4.8 collective-permute-start.3
  357.9 300.2 %all-gather.13.cloned.1.call-start = ((), (), s32[]{:S(2)}) async-start(), calls=%async_computation.14 | async-start | bytes 1810432 | tf_op jit(solution)/shard_map/all_gather | solution.py:11
  367.8 1.0 copy-start.14
  368.4 1.8 copy-start.13
  370.2 1.4 copy-start.12
  371.6 1.4 copy-start.11
  373.1 1.4 copy-start.10
  374.5 1.4 copy-start.9
  387.1 34.5 %copy-start.5 = (bf16[384,512]{1,0:T(8,128)(2,1)S(1)}, bf16[384,512]{1,0:T(8,128)(2,1)}, u32[]{:S(2)}) copy-start(bf16[384,512]{1,0:T(8,128)(2,1)} %param.15) | copy-start | bytes 1179652
  387.1 34.5 %copy-start.8 = (bf16[512,384]{0,1:T(8,128)(2,1)S(1)}, bf16[512,384]{0,1:T(8,128)(2,1)}, u32[]{:S(2)}) copy-start(bf16[512,384]{0,1:T(8,128)(2,1)} %reduce-scatter.8.cloned.1.call-done) | copy-start | bytes 1179652
  421.6 5.9 copy-start.15
  428.8 306.6 %reduce-scatter.14.cloned.1.call-start = ((), (), s32[]{:S(2)}) async-start(), calls=%async_computation.13 | async-start | bytes 8912896 | tf_op jit(solution)/shard_map/reduce_scatter | solution.py:92
  439.4 1.9 copy-start.16
  439.5 371.6 %reduce-scatter.12.cloned.1.call-start = ((), (), s32[]{:S(2)}) async-start(), calls=%async_computation.12 | async-start | bytes 8912896 | tf_op jit(solution)/shard_map/reduce_scatter | solution.py:96
  449.2 54.3 %copy-start.6 = (bf16[384,512]{1,0:T(8,128)(2,1)S(1)}, bf16[384,512]{1,0:T(8,128)(2,1)}, u32[]{:S(2)}) copy-start(bf16[384,512]{1,0:T(8,128)(2,1)} %fusion.46) | copy-start | bytes 1179652
  659.9 153.3 %copy-start.1 = (bf16[4096,30]{0,1:T(8,128)(2,1)S(1)}, bf16[4096,30]{0,1:T(8,128)(2,1)}, u32[]{:S(2)}) copy-start(bf16[4096,30]{0,1:T(8,128)(2,1)} %param.12) | copy-start | bytes 737284
Sparse Core Ops, SparseCore 0:
  10.8 66.5 all-gather.6
  79.5 61.8 all-gather.10
  144.2 61.8 all-gather.8
  226.5 77.2 reduce-scatter.7
  343.3 78.2 reduce-scatter.9
  425.3 78.1 reduce-scatter.5
  506.0 115.1 all-reduce.1
  623.6 34.5 all-gather.12
  660.7 74.6 reduce-scatter.13
  737.8 73.2 reduce-scatter.11
